TPU v7x, 32 devices: a whole 2x2x4 slice. The times are simulated.
32 devices in a mesh: seq: 8 (over y, x, core), fsdp: 4 (over z).
Axes of the slice: x: 2, y: 2, z: 4, core: 2. Of those that a mesh axis runs over, the one named last changes fastest.
Arguments:
- tokens: bfloat16 [4096, 1024], P(('seq', 'fsdp')), may hold values from -6 to 6
- first_gain: float32 [1024], P(('seq', 'fsdp')), may hold values from 0.5 to 1.5
- first_bias: float32 [1024], P(('seq', 'fsdp')), may hold values from -0.5 to 0.5
- w_qkv: float32 [1024, 3072], P(('seq', 'fsdp')), may hold values from -0.1875 to 0.1875
- query_bias: float32 [1024], P(('seq', 'fsdp')), may hold values from -0.5 to 0.5
- value_bias: float32 [1024], P(('seq', 'fsdp')), may hold values from -0.5 to 0.5
- w_proj: float32 [1024, 1024], P(('seq', 'fsdp')), may hold values from -0.75 to 0.75
- proj_bias: float32 [1024], P(('seq', 'fsdp')), may hold values from -0.5 to 0.5
- second_gain: float32 [1024], P(('seq', 'fsdp')), may hold values from 0.5 to 1.5
- second_bias: float32 [1024], P(('seq', 'fsdp')), may hold values from -0.5 to 0.5
- w_up: float32 [1024, 4096], P(('seq', 'fsdp')), may hold values from -0.1875 to 0.1875
- up_bias: float32 [4096], P(('seq', 'fsdp')), may hold values from -0.5 to 0.5
- w_down: float32 [4096, 1024], P(('seq', 'fsdp')), may hold values from -0.09375 to 0.09375
- down_bias: float32 [1024], P(('seq', 'fsdp')), may hold values from -0.5 to 0.5
- cotangent: bfloat16 [4096, 1024], P(('seq', 'fsdp')), may hold values from -6 to 6
- seq_ids: int32 [4096], P(('seq', 'fsdp')), may hold values from 0 to 31, as said below
- offsets: int32 [4096], P(('seq', 'fsdp')), may hold values from 0 to 511, as said below
Outputs:
- output: bfloat16 [4096, 1024], P(('seq', 'fsdp'))
- grad_tokens: bfloat16 [4096, 1024], P(('seq', 'fsdp'))
- grad_first_gain: float32 [1024], P(('seq', 'fsdp'))
- grad_first_bias: float32 [1024], P(('seq', 'fsdp'))
- grad_w_qkv: float32 [1024, 3072], P(('seq', 'fsdp'))
- grad_query_bias: float32 [1024], P(('seq', 'fsdp'))
- grad_value_bias: float32 [1024], P(('seq', 'fsdp'))
- grad_w_proj: float32 [1024, 1024], P(('seq', 'fsdp'))
- grad_proj_bias: float32 [1024], P(('seq', 'fsdp'))
- grad_second_gain: float32 [1024], P(('seq', 'fsdp'))
- grad_second_bias: float32 [1024], P(('seq', 'fsdp'))
- grad_w_up: float32 [1024, 4096], P(('seq', 'fsdp'))
- grad_up_bias: float32 [4096], P(('seq', 'fsdp'))
- grad_w_down: float32 [4096, 1024], P(('seq', 'fsdp'))
- grad_down_bias: float32 [1024], P(('seq', 'fsdp'))
Inputs may be any that keep to these rules, and one draw needn't show every extreme that they name: `seq_ids`: rows come in aligned blocks of 512 rows, each held by one group of fsdp devices; no sequence crosses a block. Half of the blocks, rounded up, hold one sequence of 512 rows; the others hold four sequences of 128 rows. Equal ids mark one sequence. `offsets`: the place of each row in its sequence, counting from 0.
All inputs are finite; a program needn't handle non-finite values.
Results may differ from a plain program's by a relative error of at most 0.012.
Values may be sent and summed in bfloat16 or wider, within the bound.
No kernel may reach another device: no remote copies, remote signals or barrier semaphores. Data moves between devices by JAX's collectives and lax.ppermute only.
A program may use at most 128 MiB of HBM per device.

v0:
```python
import math
import jax
import jax.numpy as jnp
from jax import lax
from jax.sharding import PartitionSpec as P

HEADS = 16
HDIM = 64
EPSILON = 1e-05


def layer_norm(values, gain, bias):
    centred = values - jnp.mean(values, axis=-1, keepdims=True)
    spread = jnp.mean(centred * centred, axis=-1, keepdims=True)
    return centred * lax.rsqrt(spread + EPSILON) * gain + bias


def gelu_tanh(values):
    return jax.nn.gelu(values, approximate=True)


def rows_dot(left, right):
    return lax.dot_general(
        left, right, (((0,), (0,)), ((), ())), preferred_element_type=jnp.float32
    )


def dot_back(left, right):
    return lax.dot_general(
        left, right, (((1,), (1,)), ((), ())), preferred_element_type=jnp.float32
    )


def gather_weights(w_qkv, w_proj, w_up, w_down):
    attn_pair = (
        lax.all_gather(w_qkv.astype(jnp.bfloat16), ("seq", "fsdp"), axis=0, tiled=True),
        lax.all_gather(w_proj.astype(jnp.bfloat16), ("seq", "fsdp"), axis=0, tiled=True),
    )
    mlp_pair = (
        lax.all_gather(w_up.astype(jnp.bfloat16), ("seq", "fsdp"), axis=0, tiled=True),
        lax.all_gather(w_down.astype(jnp.bfloat16), ("seq", "fsdp"), axis=0, tiled=True),
    )
    return (attn_pair[0], attn_pair[1], mlp_pair[0], mlp_pair[1])


def head_scores(queries, all_keys, visible):
    query_heads = queries.reshape(queries.shape[0], HEADS, HDIM)
    key_heads = all_keys.reshape(all_keys.shape[0], HEADS, HDIM)
    scores = jnp.einsum(
        "qhd,khd->hqk", query_heads, key_heads, preferred_element_type=jnp.float32
    ) * (1.0 / math.sqrt(HDIM))
    return jnp.where(visible[None], scores, jnp.float32(-1e30))


def forward_pass(tokens_f32, vectors, weights, seq_ids, offsets):
    (
        first_gain,
        first_bias,
        query_bias,
        value_bias,
        proj_bias,
        second_gain,
        second_bias,
        up_bias,
        down_bias,
    ) = vectors
    whole_qkv, whole_proj, whole_up, whole_down = weights
    model_width = tokens_f32.shape[1]
    normed = layer_norm(tokens_f32, first_gain, first_bias).astype(jnp.bfloat16)
    joined = jnp.dot(normed, whole_qkv, preferred_element_type=jnp.float32)
    queries = (joined[:, :model_width] + query_bias).astype(jnp.bfloat16)
    key_rows = joined[:, model_width : 2 * model_width].astype(jnp.bfloat16)
    value_rows = (joined[:, 2 * model_width :] + value_bias).astype(jnp.bfloat16)
    all_keys, all_values, key_ids, key_places = (
        lax.all_gather(key_rows, "fsdp", axis=0, tiled=True),
        lax.all_gather(value_rows, "fsdp", axis=0, tiled=True),
        lax.all_gather(seq_ids, "fsdp", axis=0, tiled=True),
        lax.all_gather(offsets, "fsdp", axis=0, tiled=True),
    )
    visible = (seq_ids[:, None] == key_ids[None, :]) & (key_places[None, :] <= offsets[:, None])
    scores = head_scores(queries, all_keys, visible)
    row_max = jnp.max(scores, axis=-1, keepdims=True)
    shifted = jnp.exp(scores - row_max)
    row_total = jnp.sum(shifted, axis=-1, keepdims=True)
    softmax_w = (shifted / row_total).astype(jnp.bfloat16)
    log_total = row_max + jnp.log(row_total)
    value_heads = all_values.reshape(all_values.shape[0], HEADS, HDIM)
    mixed_heads = jnp.einsum(
        "hqk,khd->qhd", softmax_w, value_heads, preferred_element_type=jnp.float32
    )
    mixed_heads = mixed_heads.reshape(queries.shape[0], model_width).astype(jnp.bfloat16)
    middle = (
        tokens_f32
        + jnp.dot(mixed_heads, whole_proj, preferred_element_type=jnp.float32)
        + proj_bias
    )
    second_normed = layer_norm(middle, second_gain, second_bias).astype(jnp.bfloat16)
    preact = jnp.dot(second_normed, whole_up, preferred_element_type=jnp.float32) + up_bias
    activated = gelu_tanh(preact).astype(jnp.bfloat16)
    result = middle + jnp.dot(activated, whole_down, preferred_element_type=jnp.float32) + down_bias
    return (
        result.astype(jnp.bfloat16),
        normed,
        queries,
        all_keys,
        all_values,
        visible,
        log_total,
        mixed_heads,
        middle,
        second_normed,
        preact,
        activated,
    )


def on_device(
    tokens,
    first_gain,
    first_bias,
    w_qkv,
    query_bias,
    value_bias,
    w_proj,
    proj_bias,
    second_gain,
    second_bias,
    w_up,
    up_bias,
    w_down,
    down_bias,
    cotangent,
    seq_ids,
    offsets,
):
    vectors = (
        lax.all_gather(first_gain, ("seq", "fsdp"), axis=0, tiled=True),
        lax.all_gather(first_bias, ("seq", "fsdp"), axis=0, tiled=True),
        lax.all_gather(query_bias, ("seq", "fsdp"), axis=0, tiled=True),
        lax.all_gather(value_bias, ("seq", "fsdp"), axis=0, tiled=True),
        lax.all_gather(proj_bias, ("seq", "fsdp"), axis=0, tiled=True),
        lax.all_gather(second_gain, ("seq", "fsdp"), axis=0, tiled=True),
        lax.all_gather(second_bias, ("seq", "fsdp"), axis=0, tiled=True),
        lax.all_gather(up_bias, ("seq", "fsdp"), axis=0, tiled=True),
        lax.all_gather(down_bias, ("seq", "fsdp"), axis=0, tiled=True),
    )
    tokens_f32 = tokens.astype(jnp.float32)
    weights = gather_weights(w_qkv, w_proj, w_up, w_down)
    stored = forward_pass(tokens_f32, vectors, weights, seq_ids, offsets)
    output = stored[0]
    weights = gather_weights(w_qkv, w_proj, w_up, w_down)
    stored = forward_pass(tokens_f32, vectors, weights, seq_ids, offsets)
    whole_qkv, whole_proj, whole_up, whole_down = weights
    (
        normed,
        queries,
        all_keys,
        all_values,
        visible,
        log_total,
        mixed_heads,
        middle,
        second_normed,
        preact,
        activated,
    ) = stored[1:]
    first_full, first_shift = (vectors[0], vectors[1])
    second_full, second_shift = (vectors[5], vectors[6])
    upstream = cotangent.astype(jnp.float32)
    row_count = tokens.shape[0]
    model_width = tokens.shape[1]
    grad_w_down = lax.psum_scatter(
        rows_dot(activated, cotangent), ("seq", "fsdp"), scatter_dimension=0, tiled=True
    )
    grad_act = dot_back(cotangent, whole_down)
    gelu_back = jax.vjp(gelu_tanh, preact)[1]
    grad_preact = gelu_back(grad_act)[0].astype(jnp.bfloat16)
    grad_w_up = lax.psum_scatter(
        rows_dot(second_normed, grad_preact), ("seq", "fsdp"), scatter_dimension=0, tiled=True
    )
    grad_second = dot_back(grad_preact, whole_up)
    second_back = jax.vjp(layer_norm, middle, second_full, second_shift)[1]
    grad_mid_norm, grad_second_gain, grad_second_bias = second_back(grad_second)
    grad_middle = upstream + grad_mid_norm
    grad_attended = grad_middle.astype(jnp.bfloat16)
    grad_w_proj = lax.psum_scatter(
        rows_dot(mixed_heads, grad_attended), ("seq", "fsdp"), scatter_dimension=0, tiled=True
    )
    grad_mixed = dot_back(grad_attended, whole_proj).astype(jnp.bfloat16)
    mixed_grad_heads = grad_mixed.reshape(row_count, HEADS, HDIM)
    value_heads = all_values.reshape(all_values.shape[0], HEADS, HDIM)
    key_heads = all_keys.reshape(all_keys.shape[0], HEADS, HDIM)
    query_heads = queries.reshape(row_count, HEADS, HDIM)
    scores = head_scores(queries, all_keys, visible)
    softmax_f = jnp.exp(scores - log_total)
    grad_probs = jnp.einsum(
        "qhd,khd->hqk", mixed_grad_heads, value_heads, preferred_element_type=jnp.float32
    )
    row_delta = jnp.sum(grad_probs * softmax_f, axis=-1, keepdims=True)
    grad_scores = (softmax_f * (grad_probs - row_delta)).astype(jnp.bfloat16)
    score_scale = 1.0 / math.sqrt(HDIM)
    grad_queries = (
        jnp.einsum("hqk,khd->qhd", grad_scores, key_heads, preferred_element_type=jnp.float32)
        * score_scale
    )
    grad_queries = grad_queries.reshape(row_count, model_width).astype(jnp.bfloat16)
    key_part = (
        jnp.einsum("hqk,qhd->khd", grad_scores, query_heads, preferred_element_type=jnp.float32)
        * score_scale
    )
    value_part = jnp.einsum(
        "hqk,qhd->khd",
        softmax_f.astype(jnp.bfloat16),
        mixed_grad_heads,
        preferred_element_type=jnp.float32,
    )
    key_count = all_keys.shape[0]
    grad_keys, grad_values = (
        lax.psum_scatter(
            key_part.reshape(key_count, model_width).astype(jnp.bfloat16),
            "fsdp",
            scatter_dimension=0,
            tiled=True,
        ).astype(jnp.float32),
        lax.psum_scatter(
            value_part.reshape(key_count, model_width).astype(jnp.bfloat16),
            "fsdp",
            scatter_dimension=0,
            tiled=True,
        ).astype(jnp.float32),
    )
    grad_keys = grad_keys.astype(jnp.bfloat16)
    grad_values = grad_values.astype(jnp.bfloat16)
    grad_joined = jnp.concatenate([grad_queries, grad_keys, grad_values], axis=1)
    grad_w_qkv = lax.psum_scatter(
        rows_dot(normed, grad_joined), ("seq", "fsdp"), scatter_dimension=0, tiled=True
    )
    grad_first = dot_back(grad_joined, whole_qkv)
    first_back = jax.vjp(layer_norm, tokens_f32, first_full, first_shift)[1]
    grad_tok_norm, grad_first_gain, grad_first_bias = first_back(grad_first)
    grad_tokens = (grad_middle + grad_tok_norm).astype(jnp.bfloat16)
    vector_sums = (
        lax.psum_scatter(grad_first_gain, ("seq", "fsdp"), scatter_dimension=0, tiled=True),
        lax.psum_scatter(grad_first_bias, ("seq", "fsdp"), scatter_dimension=0, tiled=True),
        lax.psum_scatter(
            jnp.sum(grad_queries.astype(jnp.float32), axis=0),
            ("seq", "fsdp"),
            scatter_dimension=0,
            tiled=True,
        ),
        lax.psum_scatter(
            jnp.sum(grad_values.astype(jnp.float32), axis=0),
            ("seq", "fsdp"),
            scatter_dimension=0,
            tiled=True,
        ),
        lax.psum_scatter(
            jnp.sum(grad_attended.astype(jnp.float32), axis=0),
            ("seq", "fsdp"),
            scatter_dimension=0,
            tiled=True,
        ),
        lax.psum_scatter(grad_second_gain, ("seq", "fsdp"), scatter_dimension=0, tiled=True),
        lax.psum_scatter(grad_second_bias, ("seq", "fsdp"), scatter_dimension=0, tiled=True),
        lax.psum_scatter(
            jnp.sum(grad_preact.astype(jnp.float32), axis=0),
            ("seq", "fsdp"),
            scatter_dimension=0,
            tiled=True,
        ),
        lax.psum_scatter(
            jnp.sum(upstream, axis=0), ("seq", "fsdp"), scatter_dimension=0, tiled=True
        ),
    )
    return (
        output,
        grad_tokens,
        vector_sums[0],
        vector_sums[1],
        grad_w_qkv,
        vector_sums[2],
        vector_sums[3],
        grad_w_proj,
        vector_sums[4],
        vector_sums[5],
        vector_sums[6],
        grad_w_up,
        vector_sums[7],
        grad_w_down,
        vector_sums[8],
    )


def solution(mesh):
    placed = (
        P(("seq", "fsdp"), None),
        P(("seq", "fsdp")),
        P(("seq", "fsdp")),
        P(("seq", "fsdp"), None),
        P(("seq", "fsdp")),
        P(("seq", "fsdp")),
        P(("seq", "fsdp"), None),
        P(("seq", "fsdp")),
        P(("seq", "fsdp")),
        P(("seq", "fsdp")),
        P(("seq", "fsdp"), None),
        P(("seq", "fsdp")),
        P(("seq", "fsdp"), None),
        P(("seq", "fsdp")),
        P(("seq", "fsdp"), None),
        P(("seq", "fsdp")),
        P(("seq", "fsdp")),
    )
    return jax.shard_map(
        on_device,
        mesh=mesh,
        in_specs=placed,
        out_specs=(
            P(("seq", "fsdp"), None),
            P(("seq", "fsdp"), None),
            P(("seq", "fsdp")),
            P(("seq", "fsdp")),
            P(("seq", "fsdp"), None),
            P(("seq", "fsdp")),
            P(("seq", "fsdp")),
            P(("seq", "fsdp"), None),
            P(("seq", "fsdp")),
            P(("seq", "fsdp")),
            P(("seq", "fsdp")),
            P(("seq", "fsdp"), None),
            P(("seq", "fsdp")),
            P(("seq", "fsdp"), None),
            P(("seq", "fsdp")),
        ),
        check_vma=False,
    )
```

profile of v0, /device:TPU:0, one launch (start us, length us, event | category | flops | bytes accessed | tf_op | source)
XLA Modules:
  0.0 1482.5 jit_solution(7892040546038730555)
XLA Ops:
  7.2 1.7 convert_element_type.128
  9.0 0.9 dynamic-update-slice.5
  14.9 42.7 %all-reduce.18 = (f32[1024]{0:T(1024)S(1)}, f32[1024]{0:T(1024)S(1)}, f32[1024]{0:T(1024)S(1)}, f32[1024]{0:T(1024)S(1)}, f32[1024]{0:T(1024)S(1)}, /*index=5*/f32[1024]{0:T(1024)S(1)}, f32[1024]{0:T(1024)S(1)}) all-reduce(f32[1024]{0:T(1024)S(1)} %dynamic-update-slice.1, ...), channel_id=1, replica_groups=mesh['seq'=8,'fsdp'=4] {'seq','fsdp'}, use_global_device_ids=true, to_apply=%add.1 | all-reduce | flops 7168 | bytes 57344
  57.6 1.1 convert_reduce_fusion.1
  58.7 1.2 fusion.30
  59.8 23.8 %all-gather.10.cloned.1.call-done = bf16[1024,3072]{1,0:T(8,128)(2,1)} async-done(((bf16[32,3072]{1,0:T(8,128)(2,1)}), bf16[1024,3072]{1,0:T(8,128)(2,1)}) %all-gather.10.cloned.1.call-update) | async-done | bytes 6291472 | tf_op jit(solution)/shard_map/all_gather | solution.py:36
  83.7 4.0 fusion.42
  91.7 9.6 all-gather.1
  101.3 8.0 all-gather
  109.3 65.8 %all-gather.2 = f32[32,1,128]{2,1,0:T(1,128)S(1)} all-gather(f32[1,1,128]{2,1,0:T(1,128)S(1)} %bitcast.69), channel_id=1, replica_groups=mesh['seq'=8,'fsdp'=4] {'seq','fsdp'}, dimensions={0}, use_global_device_ids=true | all-gather | bytes 16896 | tf_op jit(solution)/shard_map/all_gather | solution.py:144
  175.5 1.6 copy.44
  177.1 1.5 copy.46
  178.6 0.9 fusion.51
  179.6 1.2 fusion
  181.5 1.7 fusion.20
  183.2 20.8 %all-gather.16.cloned.1.call-done = bf16[1024,1024]{1,0:T(8,128)(2,1)} async-done(((bf16[32,1024]{1,0:T(8,128)(2,1)}), bf16[1024,1024]{1,0:T(8,128)(2,1)}) %all-gather.16.cloned.1.call-update) | async-done | bytes 2097168 | tf_op jit(solution)/shard_map/all_gather | solution.py:37
  204.0 2.1 fusion.52
  206.4 76.9 %all-gather.20.cloned.1.call-done = bf16[4096,1024]{1,0:T(8,128)(2,1)} async-done(((bf16[128,1024]{1,0:T(8,128)(2,1)}), bf16[4096,1024]{1,0:T(8,128)(2,1)}) %all-gather.20.cloned.1.call-update) | async-done | bytes 8388624 | tf_op jit(solution)/shard_map/all_gather | solution.py:41
  283.3 7.5 fusion.53
  290.8 71.6 %all-gather.18.cloned.1.call-done = bf16[1024,4096]{1,0:T(8,128)(2,1)} async-done(((bf16[32,4096]{1,0:T(8,128)(2,1)}), bf16[1024,4096]{1,0:T(8,128)(2,1)}) %all-gather.18.cloned.1.call-update) | async-done | bytes 8388624 | tf_op jit(solution)/shard_map/all_gather | solution.py:40
  362.4 8.4 convert_reduce_fusion
  370.8 3.0 multiply_reduce_fusion.1
  374.4 1.2 copy-done.4
  376.6 4.2 fusion.13
  380.8 2.3 copy.50
  383.1 3.8 multiply_reduce_fusion
  386.9 1.0 multiply_convert_fusion
  387.9 1.4 multiply_convert_fusion.1
  389.4 2.3 copy.48
  392.0 3.8 fusion.54
  395.9 2.8 convert_reduce_fusion.5
  398.6 10.5 reduce-scatter.21.cloned.1.call-done
  409.1 1.1 copy.51
  410.3 27.0 %reduce-scatter.19.cloned.1.call-done = bf16[128,1024]{1,0:T(8,128)(2,1)} async-done(((bf16[512,1024]{1,0:T(8,128)(2,1)}), bf16[128,1024]{1,0:T(8,128)(2,1)}) %reduce-scatter.19.cloned.1.call-update) | async-done | bytes 262160
  437.2 1.1 copy.49
  438.4 7.5 fusion.35
  445.9 0.9 copy-done.9
  446.8 9.7 fusion.46
  456.6 1.1 copy-done.7
  457.7 8.2 fusion.45
  467.0 5.1 fusion.47
  472.4 1.0 add_convert_fusion
  473.4 40.2 %all-reduce.17 = (f32[1024]{0:T(1024)S(1)}, f32[1024]{0:T(1024)S(1)}, f32[1024]{0:T(1024)S(1)}, f32[1024]{0:T(1024)S(1)}, f32[1024]{0:T(1024)S(1)}, /*index=5*/f...) all-reduce(f32[1024]{0:T(1024)S(1)} %dynamic-update-slice.7, ...), channel_id=1, replica_groups=mesh['seq'=8,'fsdp'=4] {'seq','fsdp'}, use_global_device_ids=true, to_apply=%add.7 | all-reduce | flops 13312 | bytes 106496
  518.8 6.3 fusion.18
  525.2 63.4 %reduce-scatter.13.cloned.1.call-done = f32[32,1024]{1,0:T(8,128)} async-done(((f32[1024,1024]{1,0:T(8,128)}), f32[32,1024]{1,0:T(8,128)}) %reduce-scatter.13.cloned.1.call-update) | async-done | bytes 131088 | tf_op jit(solution)/shard_map/reduce_scatter | solution.py:186
  588.6 159.9 %reduce-scatter.11.cloned.1.call-done = f32[32,3072]{1,0:T(8,128)} async-done(((f32[1024,3072]{1,0:T(8,128)}), f32[32,3072]{1,0:T(8,128)}) %reduce-scatter.11.cloned.1.call-update) | async-done | bytes 393232 | tf_op jit(solution)/shard_map/reduce_scatter | solution.py:235
  748.4 362.5 %reduce-scatter.17.cloned.1.call-done = f32[128,1024]{1,0:T(8,128)} async-done(((f32[4096,1024]{1,0:T(8,128)}), f32[128,1024]{1,0:T(8,128)}) %reduce-scatter.17.cloned.1.call-update) | async-done | bytes 524304 | tf_op jit(solution)/shard_map/reduce_scatter | solution.py:172
  1110.9 364.7 %reduce-scatter.15.cloned.1.call-done = f32[32,4096]{1,0:T(8,128)} async-done(((f32[1024,4096]{1,0:T(8,128)}), f32[32,4096]{1,0:T(8,128)}) %reduce-scatter.15.cloned.1.call-update) | async-done | bytes 524304 | tf_op jit(solution)/shard_map/reduce_scatter | solution.py:178
  (119 shorter events, 19.1 us)
Async XLA Ops:
  7.2 76.5 %all-gather.10.cloned.1.call-start = ((), (), s32[]{:S(2)}) async-start(), calls=%async_computation.6 | async-start | bytes 6488064 | tf_op jit(solution)/shard_map/all_gather | solution.py:36
  8.9 166.5 %all-gather.12.cloned.1.call-start = ((), (), s32[]{:S(2)}) async-start(), calls=%async_computation.7 | async-start | bytes 1310720 | tf_op jit(solution)/shard_map/all_gather | solution.py:76
  87.6 1.7 copy-start.19
  87.6 2.5 copy-start.17
  87.6 3.3 copy-start.18
  88.5 3.3 copy-start.20
  88.5 12.8 copy-start.21
  88.5 20.8 %copy-start.22 = (f32[128]{0:T(128)S(1)}, f32[128]{0:T(128)}, u32[]{:S(2)}) copy-start(f32[128]{0:T(128)} %param.28) | copy-start | bytes 1540
  88.5 88.6 %all-gather.14.cloned.1.call-start = ((), (), s32[]{:S(2)}) async-start(), calls=%async_computation.8 | async-start | bytes 1310720 | tf_op jit(solution)/shard_map/all_gather | solution.py:75
  89.3 114.7 %all-gather.16.cloned.1.call-start = ((), (), s32[]{:S(2)}) async-start(), calls=%async_computation.9 | async-start | bytes 2162688 | tf_op jit(solution)/shard_map/all_gather | solution.py:37
  90.0 193.3 %all-gather.20.cloned.1.call-start = ((), (), s32[]{:S(2)}) async-start(), calls=%async_computation.11 | async-start | bytes 8650752 | tf_op jit(solution)/shard_map/all_gather | solution.py:41
  90.9 271.5 %all-gather.18.cloned.1.call-start = ((), (), s32[]{:S(2)}) async-start(), calls=%async_computation.10 | async-start | bytes 8650752 | tf_op jit(solution)/shard_map/all_gather | solution.py:40
  91.7 317.5 %reduce-scatter.21.cloned.1.call-start = ((), (), s32[]{:S(2)}) async-start(), calls=%async_computation.17 | async-start | bytes 1310720
  175.4 3.2 copy-start.11
  178.6 1.0 copy-start.3
  179.5 2.0 copy-start
  181.5 22.5 %copy-start.2 = (bf16[128,1024]{1,0:T(8,128)(2,1)S(1)}, bf16[128,1024]{1,0:T(8,128)(2,1)}, u32[]{:S(2)}) copy-start(bf16[128,1024]{1,0:T(8,128)(2,1)} %param.17) | copy-start | bytes 786436
  183.2 107.7 %copy-start.15 = (bf16[16,64,128]{2,1,0:T(8,128)(2,1)}, bf16[16,64,128]{2,1,0:T(8,128)(2,1)S(1)}, u32[]{:S(2)}) copy-start(bf16[16,64,128]{2,1,0:T(8,128)(2,1)S(1)} %fusion.20) | copy-start | bytes 786436
  183.2 100.1 %copy-start.8 = (bf16[128,1024]{1,0:T(8,128)(2,1)S(1)}, bf16[128,1024]{1,0:T(8,128)(2,1)}, u32[]{:S(2)}) copy-start(bf16[128,1024]{1,0:T(8,128)(2,1)} %param.31) | copy-start | bytes 786436
  362.4 8.4 copy-start.5
  370.8 3.0 copy-start.6
  373.9 1.7 copy-start.4
  374.3 6.4 copy-start.10
  383.1 54.2 %reduce-scatter.19.cloned.1.call-start = ((), (), s32[]{:S(2)}) async-start(), calls=%async_computation.16 | async-start | bytes 1310720
  383.1 3.8 copy-start.1
  386.9 1.0 copy-start.12
  391.7 196.9 %reduce-scatter.13.cloned.1.call-start = ((), (), s32[]{:S(2)}) async-start(), calls=%async_computation.13 | async-start | bytes 4325376 | tf_op jit(solution)/shard_map/reduce_scatter | solution.py:186
  395.8 352.6 %reduce-scatter.11.cloned.1.call-start = ((), (), s32[]{:S(2)}) async-start(), calls=%async_computation.12 | async-start | bytes 12976128 | tf_op jit(solution)/shard_map/reduce_scatter | solution.py:235
  438.4 7.5 copy-start.13
  445.9 1.0 copy-start.9
  445.9 665.0 %reduce-scatter.17.cloned.1.call-start = ((), (), s32[]{:S(2)}) async-start(), calls=%async_computation.15 | async-start | bytes 17301504 | tf_op jit(solution)/shard_map/reduce_scatter | solution.py:172
  456.5 1.2 copy-start.7
  456.5 1019.1 %reduce-scatter.15.cloned.1.call-start = ((), (), s32[]{:S(2)}) async-start(), calls=%async_computation.14 | async-start | bytes 17301504 | tf_op jit(solution)/shard_map/reduce_scatter | solution.py:178
  465.9 0.7 copy-start.23
  465.9 1.0 copy-start.14
  465.9 1.1 copy-start.16
Sparse Core Ops, SparseCore 0:
  11.4 72.1 all-gather.9
  88.6 26.5 all-gather.11
  117.4 27.4 all-gather.13
  148.2 55.7 all-gather.15
  207.3 75.9 all-gather.19
  286.7 75.6 all-gather.17
  383.2 25.9 reduce-scatter.20
  411.4 25.7 reduce-scatter.18
  440.1 148.4 reduce-scatter.12
  595.0 153.3 reduce-scatter.10
  751.3 359.5 reduce-scatter.16
  1113.6 361.9 reduce-scatter.14
where the time goes:
time: 1480 us
  waiting for transfers between devices  1180 us (80%)
  blocking collectives  166 us (11%)
  matrix products  81.2 us (5%)
  local copies, waits for them, and re-layouts  27 us (2%)
    reduce_scatter x1, waiting for transfers between devices, on_device(): lax.psum_scatter(rows_dot(second_normed, grad_preact), ('seq', 'fsdp'), s...  365 us
    reduce_scatter x1, waiting for transfers between devices, on_device(): lax.psum_scatter(rows_dot(activated, cotangent), ('seq', 'fsdp'), scatter...  362 us
    reduce_scatter x1, waiting for transfers between devices, on_device(): lax.psum_scatter(rows_dot(normed, grad_joined), ('seq', 'fsdp'), scatter_...  160 us
    unnamed x2, blocking collectives  82.9 us
    all_gather x1, waiting for transfers between devices, gather_weights(): lax.all_gather(w_down.astype(jnp.bfloat16), ('seq', 'fsdp'), axis=0, tile...  76.9 us
    all_gather x1, waiting for transfers between devices, gather_weights(): lax.all_gather(w_up.astype(jnp.bfloat16), ('seq', 'fsdp'), axis=0, tiled=...  71.6 us
    all_gather x1, blocking collectives, on_device(): lax.all_gather(up_bias, ('seq', 'fsdp'), axis=0, tiled=True)  65.8 us
    reduce_scatter x1, waiting for transfers between devices, on_device(): lax.psum_scatter(rows_dot(mixed_heads, grad_attended), ('seq', 'fsdp'), s...  63.4 us
  transfers between devices with their start and end apart: 12, of which 10 were waited for; matrix products, arithmetic and copies ran while one was open for 6% of the time, Pallas kernels for 0%

commit v1 on v0

--- a/solution.py
+++ b/solution.py
@@ -1,3 +1,4 @@
+import functools
 import math
 import jax
 import jax.numpy as jnp
@@ -7,6 +8,21 @@
 HEADS = 16
 HDIM = 64
 EPSILON = 1e-05
+
+
+def order_group(sheet, axis_k):
+    after, part_now = (lax.psum(1, ("seq", "fsdp")), lax.axis_index(("seq", "fsdp")))
+    f_now, w1 = (sheet, 1)
+    while w1 < after:
+        y = lax.ppermute(f_now, ("seq", "fsdp"), [(ix, ix ^ w1) for ix in range(after)])
+        top = jnp.concatenate([f_now, y], axis=axis_k)
+        earlier = jnp.concatenate([y, f_now], axis=axis_k)
+        f_now = jnp.where(part_now & w1 == 0, top, earlier)
+        w1 = 2 * w1
+    return f_now
+
+
+replace_strings = functools.partial(order_group, axis_k=0)
 
 
 def layer_norm(values, gain, bias):
@@ -141,7 +157,7 @@
         lax.all_gather(proj_bias, ("seq", "fsdp"), axis=0, tiled=True),
         lax.all_gather(second_gain, ("seq", "fsdp"), axis=0, tiled=True),
         lax.all_gather(second_bias, ("seq", "fsdp"), axis=0, tiled=True),
-        lax.all_gather(up_bias, ("seq", "fsdp"), axis=0, tiled=True),
+        replace_strings(up_bias),
         lax.all_gather(down_bias, ("seq", "fsdp"), axis=0, tiled=True),
     )
     tokens_f32 = tokens.astype(jnp.float32)

time: 1480 us -> 1480 us (level)
  blocking collectives: 166 us -> 101 us
  waiting for transfers between devices: 1180 us -> 1240 us
    all_gather x1 -> x0, blocking collectives: 65.8 us -> none  [on_device(): lax.all_gather(up_bias, ('seq', 'fsdp'), axis=0, tiled=True)]
    all_gather x1, waiting for transfers between devices: 20.8 us -> 53.2 us  [gather_weights(): lax.all_gather(w_proj.astype(jnp.bfloat16), ('seq', 'fsdp'), axis=0, tile...]
    all_gather x1, waiting for transfers between devices: 0.02 us -> 19.2 us  [forward_pass(): lax.all_gather(key_rows, 'fsdp', axis=0, tiled=True)]
  transfers between devices with their start and end apart: 12 -> 17, of which waited for: 10 -> 15; matrix products, arithmetic and copies ran while one was open for 6% -> 6% of each run, Pallas kernels for 0% -> 0%
where the time goes in v1:
time: 1480 us
  waiting for transfers between devices  1240 us (84%)
  blocking collectives  101 us (7%)
  matrix products  76.4 us (5%)
  local copies, waits for them, and re-layouts  26.6 us (2%)
    reduce_scatter x1, waiting for transfers between devices, on_device(): lax.psum_scatter(rows_dot(second_normed, grad_preact), ('seq', 'fsdp'), s...  365 us
    reduce_scatter x1, waiting for transfers between devices, on_device(): lax.psum_scatter(rows_dot(activated, cotangent), ('seq', 'fsdp'), scatter...  362 us
    reduce_scatter x1, waiting for transfers between devices, on_device(): lax.psum_scatter(rows_dot(normed, grad_joined), ('seq', 'fsdp'), scatter_...  160 us
    unnamed x2, blocking collectives  83.1 us
    all_gather x1, waiting for transfers between devices, gather_weights(): lax.all_gather(w_up.astype(jnp.bfloat16), ('seq', 'fsdp'), axis=0, tiled=...  76.9 us
    all_gather x1, waiting for transfers between devices, gather_weights(): lax.all_gather(w_down.astype(jnp.bfloat16), ('seq', 'fsdp'), axis=0, tile...  74.3 us
    reduce_scatter x1, waiting for transfers between devices, on_device(): lax.psum_scatter(rows_dot(mixed_heads, grad_attended), ('seq', 'fsdp'), s...  62.1 us
    all_gather x1, waiting for transfers between devices, gather_weights(): lax.all_gather(w_proj.astype(jnp.bfloat16), ('seq', 'fsdp'), axis=0, tile...  53.2 us
  transfers between devices with their start and end apart: 17, of which 15 were waited for; matrix products, arithmetic and copies ran while one was open for 6% of the time, Pallas kernels for 0%

profile of v1, /device:TPU:0, one launch (start us, length us, event | category | flops | bytes accessed | tf_op | source)
XLA Modules:
  0.0 1479.7 jit_solution(5995670709961864967)
XLA Ops:
  7.2 1.7 convert_element_type.128
  14.9 42.7 %all-reduce.18 = (f32[1024]{0:T(1024)S(1)}, f32[1024]{0:T(1024)S(1)}, f32[1024]{0:T(1024)S(1)}, f32[1024]{0:T(1024)S(1)}, f32[1024]{0:T(1024)S(1)}, /*index=5*/f32[1024]{0:T(1024)S(1)}, f32[1024]{0:T(1024)S(1)}) all-reduce(f32[1024]{0:T(1024)S(1)} %dynamic-update-slice.1, ...), channel_id=1, replica_groups=mesh['seq'=8,'fsdp'=4] {'seq','fsdp'}, use_global_device_ids=true, to_apply=%add.1 | all-reduce | flops 7168 | bytes 57344
  58.7 1.2 fusion.30
  59.8 23.8 %all-gather.9.cloned.1.call-done = bf16[1024,3072]{1,0:T(8,128)(2,1)} async-done(((bf16[32,3072]{1,0:T(8,128)(2,1)}), bf16[1024,3072]{1,0:T(8,128)(2,1)}) %all-gather.9.cloned.1.call-update) | async-done | bytes 6291472 | tf_op jit(solution)/shard_map/all_gather | solution.py:52
  83.7 4.0 fusion.42
  91.7 1.6 collective-permute-start
  93.3 2.0 collective-permute-done
  95.4 1.8 collective-permute-start.1
  97.2 2.7 collective-permute-done.1
  99.9 1.1 collective-permute-done.2
  101.1 1.4 collective-permute-start.3
  102.5 9.9 all-gather.1
  112.4 7.6 all-gather
  120.9 2.8 collective-permute-done.4
  123.9 1.7 copy.44
  125.6 19.2 %all-gather.13.cloned.1.call-done = bf16[512,1024]{1,0:T(8,128)(2,1)} async-done(((bf16[128,1024]{1,0:T(8,128)(2,1)}), bf16[512,1024]{1,0:T(8,128)(2,1)}) %all-gather.13.cloned.1.call-update) | async-done | bytes 1048592 | tf_op jit(solution)/shard_map/all_gather | solution.py:91
  144.8 1.5 copy.46
  147.3 1.2 fusion
  149.2 1.5 fusion.20
  150.8 53.2 %all-gather.15.cloned.1.call-done = bf16[1024,1024]{1,0:T(8,128)(2,1)} async-done(((bf16[32,1024]{1,0:T(8,128)(2,1)}), bf16[1024,1024]{1,0:T(8,128)(2,1)}) %all-gather.15.cloned.1.call-update) | async-done | bytes 2097168 | tf_op jit(solution)/shard_map/all_gather | solution.py:53
  203.9 2.1 fusion.53
  206.3 76.9 %all-gather.17.cloned.1.call-done = bf16[1024,4096]{1,0:T(8,128)(2,1)} async-done(((bf16[32,4096]{1,0:T(8,128)(2,1)}), bf16[1024,4096]{1,0:T(8,128)(2,1)}) %all-gather.17.cloned.1.call-update) | async-done | bytes 8388624 | tf_op jit(solution)/shard_map/all_gather | solution.py:56
  283.2 4.8 fusion.46
  288.0 74.3 %all-gather.19.cloned.1.call-done = bf16[4096,1024]{1,0:T(8,128)(2,1)} async-done(((bf16[128,1024]{1,0:T(8,128)(2,1)}), bf16[4096,1024]{1,0:T(8,128)(2,1)}) %all-gather.19.cloned.1.call-update) | async-done | bytes 8388624 | tf_op jit(solution)/shard_map/all_gather | solution.py:57
  362.3 7.2 convert_reduce_fusion
  369.6 3.0 multiply_reduce_fusion.1
  373.1 1.2 copy-done.7
  376.1 3.1 fusion.13
  379.2 1.6 copy.50
  380.8 3.9 multiply_reduce_fusion
  385.7 1.4 multiply_convert_fusion.1
  387.2 2.3 copy.48
  389.5 3.8 fusion.54
  393.4 2.8 convert_reduce_fusion.5
  396.2 10.7 reduce-scatter.21.cloned.1.call-done
  406.8 1.1 copy.51
  408.0 27.0 %reduce-scatter.19.cloned.1.call-done = bf16[128,1024]{1,0:T(8,128)(2,1)} async-done(((bf16[512,1024]{1,0:T(8,128)(2,1)}), bf16[128,1024]{1,0:T(8,128)(2,1)}) %reduce-scatter.19.cloned.1.call-update) | async-done | bytes 262160
  436.1 7.5 fusion.35
  443.6 1.5 copy-done.5
  445.2 9.1 fusion.47
  454.3 9.4 fusion.45
  465.7 5.4 fusion.48
  472.5 40.3 %all-reduce.17 = (f32[1024]{0:T(1024)S(1)}, f32[1024]{0:T(1024)S(1)}, f32[1024]{0:T(1024)S(1)}, f32[1024]{0:T(1024)S(1)}, f32[1024]{0:T(1024)S(1)}, /*index=5*/f...) all-reduce(f32[1024]{0:T(1024)S(1)} %dynamic-update-slice.7, ...), channel_id=1, replica_groups=mesh['seq'=8,'fsdp'=4] {'seq','fsdp'}, use_global_device_ids=true, to_apply=%add.7 | all-reduce | flops 13312 | bytes 106496
  518.1 5.7 fusion.18
  523.8 62.1 %reduce-scatter.13.cloned.1.call-done = f32[32,1024]{1,0:T(8,128)} async-done(((f32[1024,1024]{1,0:T(8,128)}), f32[32,1024]{1,0:T(8,128)}) %reduce-scatter.13.cloned.1.call-update) | async-done | bytes 131088 | tf_op jit(solution)/shard_map/reduce_scatter | solution.py:202
  585.9 159.8 %reduce-scatter.11.cloned.1.call-done = f32[32,3072]{1,0:T(8,128)} async-done(((f32[1024,3072]{1,0:T(8,128)}), f32[32,3072]{1,0:T(8,128)}) %reduce-scatter.11.cloned.1.call-update) | async-done | bytes 393232 | tf_op jit(solution)/shard_map/reduce_scatter | solution.py:251
  745.7 362.5 %reduce-scatter.17.cloned.1.call-done = f32[128,1024]{1,0:T(8,128)} async-done(((f32[4096,1024]{1,0:T(8,128)}), f32[128,1024]{1,0:T(8,128)}) %reduce-scatter.17.cloned.1.call-update) | async-done | bytes 524304 | tf_op jit(solution)/shard_map/reduce_scatter | solution.py:188
  1108.2 364.7 %reduce-scatter.15.cloned.1.call-done = f32[32,4096]{1,0:T(8,128)} async-done(((f32[1024,4096]{1,0:T(8,128)}), f32[32,4096]{1,0:T(8,128)}) %reduce-scatter.15.cloned.1.call-update) | async-done | bytes 524304 | tf_op jit(solution)/shard_map/reduce_scatter | solution.py:194
  (139 shorter events, 27.2 us)
Async XLA Ops:
  7.2 76.5 %all-gather.9.cloned.1.call-start = ((), (), s32[]{:S(2)}) async-start(), calls=%async_computation.6 | async-start | bytes 6488064 | tf_op jit(solution)/shard_map/all_gather | solution.py:52
  8.9 114.9 %all-gather.11.cloned.1.call-start = ((), (), s32[]{:S(2)}) async-start(), calls=%async_computation.7 | async-start | bytes 1310720 | tf_op jit(solution)/shard_map/all_gather | solution.py:92
  87.6 1.7 copy-start.22
  87.6 2.5 copy-start.20
  87.7 3.3 copy-start.21
  88.5 3.3 copy-start.25
  88.5 14.0 copy-start.23
  88.5 23.9 %copy-start.24 = (s32[128]{0:T(128)S(1)}, s32[128]{0:T(128)}, u32[]{:S(2)}) copy-start(s32[128]{0:T(128)} %param.32) | copy-start | bytes 1540
  88.5 56.3 %all-gather.13.cloned.1.call-start = ((), (), s32[]{:S(2)}) async-start(), calls=%async_computation.8 | async-start | bytes 1310720 | tf_op jit(solution)/shard_map/all_gather | solution.py:91
  89.3 114.6 %all-gather.15.cloned.1.call-start = ((), (), s32[]{:S(2)}) async-start(), calls=%async_computation.9 | async-start | bytes 2162688 | tf_op jit(solution)/shard_map/all_gather | solution.py:53
  90.0 193.2 %all-gather.17.cloned.1.call-start = ((), (), s32[]{:S(2)}) async-start(), calls=%async_computation.10 | async-start | bytes 8650752 | tf_op jit(solution)/shard_map/all_gather | solution.py:56
  90.9 271.4 %all-gather.19.cloned.1.call-start = ((), (), s32[]{:S(2)}) async-start(), calls=%async_computation.11 | async-start | bytes 8650752 | tf_op jit(solution)/shard_map/all_gather | solution.py:57
  91.7 315.1 %reduce-scatter.21.cloned.1.call-start = ((), (), s32[]{:S(2)}) async-start(), calls=%async_computation.17 | async-start | bytes 1310720
  91.7 3.6 collective-permute-start
  95.4 4.5 collective-permute-start.1
  99.9 1.2 collective-permute-start.2
  101.1 18.9 %collective-permute-start.3 = (f32[1024]{0:T(1024)S(1)}, f32[1024]{0:T(1024)S(1)}, u32[]{:S(2)}, u32[]{:S(2)}) collective-permute-start(f32[1024]{0:T(1024)S(1)} %maximum_select_fusion.2), channel_id=1, source_target_pairs={{0,8},{1,9},{2,10},{3,11},{4,12},{5,13},{6,14},{7,15},{8,0},{9,1},... | collective-permute-start | bytes 12296 | tf_op jit(solution)/shard_map/ppermute | solution.py:17
  120.0 3.7 collective-permute-start.4
  123.8 22.4 %copy-start.15 = (bf16[128,1024]{0,1:T(8,128)(2,1)}, bf16[128,1024]{0,1:T(8,128)(2,1)S(1)}, u32[]{:S(2)}) copy-start(bf16[128,1024]{0,1:T(8,128)(2,1)S(1)} %copy.45) | copy-start | bytes 786436
  125.6 22.9 %copy-start.9 = (bf16[512,1024]{0,1:T(8,128)(2,1)}, bf16[512,1024]{0,1:T(8,128)(2,1)S(1)}, u32[]{:S(2)}) copy-start(bf16[512,1024]{0,1:T(8,128)(2,1)S(1)} %copy.44) | copy-start | bytes 3145732
  146.3 1.0 copy-start.6
  147.3 2.0 copy-start
  149.2 54.7 %copy-start.3 = (bf16[128,1024]{1,0:T(8,128)(2,1)S(1)}, bf16[128,1024]{1,0:T(8,128)(2,1)}, u32[]{:S(2)}) copy-start(bf16[128,1024]{1,0:T(8,128)(2,1)} %param.17) | copy-start | bytes 786436
  150.7 132.5 %copy-start.19 = (bf16[16,64,128]{2,1,0:T(8,128)(2,1)}, bf16[16,64,128]{2,1,0:T(8,128)(2,1)S(1)}, u32[]{:S(2)}) copy-start(bf16[16,64,128]{2,1,0:T(8,128)(2,1)S(1)} %fusion.20) | copy-start | bytes 786436
  283.2 79.1 %copy-start.11 = (bf16[128,1024]{1,0:T(8,128)(2,1)S(1)}, bf16[128,1024]{1,0:T(8,128)(2,1)}, u32[]{:S(2)}) copy-start(bf16[128,1024]{1,0:T(8,128)(2,1)} %param.31) | copy-start | bytes 786436
  288.0 81.6 %copy-start.4 = (f32[128,4096]{1,0:T(8,128)}, f32[128,4096]{1,0:T(8,128)S(1)}, u32[]{:S(2)}) copy-start(f32[128,4096]{1,0:T(8,128)S(1)} %fusion.46) | copy-start | bytes 6291460
  362.3 7.3 copy-start.2
  369.6 3.1 copy-start.8
  372.6 1.7 copy-start.7
  373.1 2.3 copy-start.14
  375.3 0.7 copy-start.17
  379.2 1.6 copy-start.10
  380.8 54.2 %reduce-scatter.19.cloned.1.call-start = ((), (), s32[]{:S(2)}) async-start(), calls=%async_computation.16 | async-start | bytes 1310720
  380.8 3.9 copy-start.1
  384.7 1.0 copy-start.16
  389.5 196.5 %reduce-scatter.13.cloned.1.call-start = ((), (), s32[]{:S(2)}) async-start(), calls=%async_computation.13 | async-start | bytes 4325376 | tf_op jit(solution)/shard_map/reduce_scatter | solution.py:202
  393.4 352.4 %reduce-scatter.11.cloned.1.call-start = ((), (), s32[]{:S(2)}) async-start(), calls=%async_computation.12 | async-start | bytes 12976128 | tf_op jit(solution)/shard_map/reduce_scatter | solution.py:251
  408.0 35.6 %copy-start.13 = (bf16[128,1024]{0,1:T(8,128)(2,1)}, bf16[128,1024]{0,1:T(8,128)(2,1)S(1)}, u32[]{:S(2)}) copy-start(bf16[128,1024]{0,1:T(8,128)(2,1)S(1)} %copy.51) | copy-start | bytes 786436
  436.1 7.5 copy-start.18
  443.6 1.6 copy-start.5
  443.6 664.6 %reduce-scatter.17.cloned.1.call-start = ((), (), s32[]{:S(2)}) async-start(), calls=%async_computation.15 | async-start | bytes 17301504 | tf_op jit(solution)/shard_map/reduce_scatter | solution.py:188
  454.2 1018.6 %reduce-scatter.15.cloned.1.call-start = ((), (), s32[]{:S(2)}) async-start(), calls=%async_computation.14 | async-start | bytes 17301504 | tf_op jit(solution)/shard_map/reduce_scatter | solution.py:194
  463.7 0.7 copy-start.26
  465.7 5.8 copy-start.12
Sparse Core Ops, SparseCore 0:
  11.4 72.1 all-gather.8
  88.6 26.5 all-gather.10
  117.4 27.3 all-gather.12
  148.1 55.7 all-gather.14
  207.3 75.9 all-gather.16
  286.6 75.6 all-gather.18
  380.9 25.9 reduce-scatter.20
  409.1 25.7 reduce-scatter.18
  437.8 148.1 reduce-scatter.12
  592.4 153.3 reduce-scatter.10
  748.6 359.5 reduce-scatter.16
  1110.9 361.9 reduce-scatter.14
